TPU v7x, 512 devices: a whole 4x4x16 slice. The times are simulated.
512 devices in a mesh: tm: 256 (over z, y, x), state: 2 (over core).
Axes of the slice: x: 4, y: 4, z: 16, core: 2. Of those that a mesh axis runs over, the one named last changes fastest.
Arguments:
- record: bfloat16 [32768, 4096], P('tm', 'state'), may hold values from -24 to 24
- gain: bfloat16 [2, 256, 4096], P(None, 'state'), may hold values from -0.0625 to 0.0625
- rate: float32 [256, 32768], P('state', 'tm'), as said below
- leak: float32 [256], P('state'), may hold values from 1.5258789e-05 to 0.05
- dilation: int32 [2], replicated, may hold values from 0 to 64, as said below
Outputs:
- smoothed: float32 [256, 32768], P('state', 'tm')
- grad: float32 [4096, 512], P(('state', 'tm'))
Inputs may be any that keep to these rules, and one draw needn't show every extreme that they name: `dilation`: delays of the taps; the largest of them equals 64. `rate`: positive rates.
All inputs are finite; a program needn't handle non-finite values.
Results may differ from a plain program's by a relative error of at most 0.0014.
Values may be sent and summed in bfloat16 or wider, within the bound.
No kernel may reach another device: no remote copies, remote signals or barrier semaphores. Data moves between devices by JAX's collectives and lax.ppermute only.
A program may use at most 64 MiB of HBM per device.

v0:
```python
import jax
import jax.numpy as jnp
from jax import lax
from jax.sharding import Mesh
from jax.sharding import PartitionSpec as P

TAPS = 2
DMAX = 64
TM = ("tm_0", "tm_1", "tm_2")
STATE_TM = ("state", "tm_0", "tm_1", "tm_2")


def from_behind(x, axis, by):
    peers = lax.axis_size(axis)
    pairs = [(i, i + by) for i in range(peers) if 0 <= i + by < peers]
    return lax.ppermute(x, axis, pairs)


def copy_for_each(x, axis):
    copies = jnp.broadcast_to(x, (lax.axis_size(axis), *x.shape))
    return lax.all_to_all(copies, axis, split_axis=0, concat_axis=0, tiled=True)


def of_everyone(x, axis):
    everything = copy_for_each(x, axis)
    return jnp.sum(everything, axis=0)


def laid_out(blocks, dim):
    blocks = jnp.moveaxis(blocks, 0, dim)
    lengths = blocks.shape
    return blocks.reshape(*lengths[:dim], lengths[dim] * lengths[dim + 1], *lengths[dim + 2 :])


def gathered_by_axis(x, axes, dim):
    far, near = axes
    blocks = copy_for_each(copy_for_each(x, far), near)
    return laid_out(blocks.swapaxes(0, 1).reshape(-1, *x.shape), dim)


def in_one_piece(arrays, axis, dim, along):
    widths = [a.shape[along] for a in arrays]
    both = jnp.concatenate(arrays, axis=along)
    whole = gathered_by_axis(both, axis, dim)
    return tuple(jnp.split(whole, [sum(widths[:k]) for k in range(1, len(widths))], axis=along))


def gather_directly(x, axis, dim):
    return laid_out(copy_for_each(x, axis), dim)


def in_blocks(x, dim, peers):
    lengths = x.shape
    blocks = x.reshape(*lengths[:dim], peers, lengths[dim] // peers, *lengths[dim + 1 :])
    return jnp.moveaxis(blocks, dim, 0)


def summed_on_arrival(x, axis, dim):
    peers = lax.axis_size(axis)
    blocks = lax.all_to_all(in_blocks(x, dim, peers), axis, 0, 0, tiled=True)
    return jnp.sum(blocks, axis=0)


def sum_by_axis(x, axes, dim):
    far, near = axes
    own = summed_on_arrival(in_blocks(x, dim, lax.axis_size(far)), near, dim + 1)
    return jnp.sum(lax.all_to_all(own, far, 0, 0, tiled=True), axis=0)


def affine(first, second):
    return (first[0] * second[0], second[0] * first[1] + second[1])


def entry_from_all(pair, backward, position, count):
    inclusive = lax.associative_scan(affine, pair, reverse=backward, axis=0)
    if backward:
        pick = position + 1
        valid = position < count - 1
    else:
        pick = position - 1
        valid = position > 0
    safe = jnp.clip(pick, 0, count - 1)
    value = lax.dynamic_index_in_dim(inclusive[1], safe, 0, keepdims=False)
    return jnp.where(valid, value, 0.0)


def running_sum(values, triangle):
    return jnp.dot(
        values, triangle, precision=lax.Precision.HIGHEST, preferred_element_type=jnp.float32
    )


def block_recursion(log_sums, inputs, keep):
    differ = jnp.where(keep[None], log_sums[:, :, None] - log_sums[:, None, :], 0.0)
    kernel = jnp.where(keep[None], jnp.exp(-jnp.abs(differ)), 0.0)
    return jnp.einsum(
        "hts,hs->ht",
        kernel,
        inputs,
        precision=lax.Precision.HIGHEST,
        preferred_element_type=jnp.float32,
    )


def per_device(record, gain, rate, leak, dilation):
    frames = record.shape[0]
    tail = record[frames - DMAX :]
    rim_rows = from_behind(tail, TM, 1)
    local_rows = jnp.concatenate([rim_rows, record], 0)
    local_taps = [
        lax.dynamic_slice_in_dim(local_rows, DMAX - dilation[k], frames, 0) for k in range(TAPS)
    ]
    gain_cols = lax.all_to_all(gain, "state", split_axis=2, concat_axis=1, tiled=True)
    local_view = jnp.stack(local_taps, 1)
    partial_drive = jnp.einsum(
        "lky,khy->hl", local_view, gain_cols, preferred_element_type=jnp.float32
    )
    total_drive = of_everyone(partial_drive, "state")
    own_modes = gain.shape[1]
    drive_in = lax.dynamic_slice_in_dim(
        total_drive, lax.axis_index("state") * own_modes, own_modes, 0
    )
    decay = jnp.exp(-rate)
    scale = jnp.sqrt(-jnp.expm1(-2.0 * rate))
    drive = scale * drive_in
    position = lax.axis_index(TM)
    count = lax.axis_size(TM)
    steps_idx = lax.iota(jnp.int32, frames)
    upper_incl = (steps_idx[:, None] <= steps_idx[None, :]).astype(jnp.float32)
    upper_excl = (steps_idx[:, None] < steps_idx[None, :]).astype(jnp.float32)
    lower_keep = steps_idx[:, None] >= steps_idx[None, :]
    upper_keep = steps_idx[:, None] <= steps_idx[None, :]
    rate_sums = running_sum(rate, upper_incl)
    offsets = block_recursion(rate_sums, drive, lower_keep)
    prods = jnp.exp(-rate_sums)
    summary = (prods[:, -1], offsets[:, -1])
    every = in_one_piece((summary[0][None], summary[1][None]), (("tm_0", "tm_1"), "tm_2"), 0, 1)
    entering = entry_from_all(every, False, position, count)
    filtered = prods * entering[:, None] + offsets
    kappa = 1.0 - leak
    weight = (1.0 - kappa[:, None] * decay * decay) * filtered
    link_rate = rate - jnp.log(kappa)[:, None]
    link_sums = running_sum(link_rate, upper_excl)
    weights = block_recursion(link_sums, weight, upper_keep)
    link_total = link_sums[:, -1:] + link_rate[:, -1:]
    links = jnp.exp(-(link_total - link_sums))
    closing = (links[:, 0], weights[:, 0])
    every_back = in_one_piece(
        (closing[0][None], closing[1][None]), (("tm_0", "tm_1"), "tm_2"), 0, 1
    )
    after = entry_from_all(every_back, True, position, count)
    smoothed = links * after[:, None] + weights
    prior = from_behind(smoothed[:, -1:], TM, 1)
    shifted = jnp.concatenate([prior, smoothed[:, :-1]], 1)
    resid = (smoothed - decay * shifted - drive).astype(jnp.bfloat16)
    resid_all = gather_directly(resid, "state", 0)
    pieces = []
    for k in range(TAPS):
        columns = local_taps[k]
        pieces.append(
            lax.dot_general(
                columns, resid_all, (((0,), (1,)), ((), ())), preferred_element_type=jnp.float32
            )
        )
    grad = sum_by_axis(jnp.concatenate(pieces, 1), (("tm_0", "tm_1"), "tm_2"), 0)
    return (smoothed, grad)


def solution(mesh):
    split = Mesh(
        mesh.devices.reshape(16, 4, 4, mesh.shape["state"]), ("tm_0", "tm_1", "tm_2", "state")
    )
    return jax.shard_map(
        per_device,
        mesh=split,
        in_specs=(P(TM, "state"), P(None, "state", None), P("state", TM), P("state"), P()),
        out_specs=(P("state", TM), P(STATE_TM, None)),
        check_vma=False,
    )
```

profile of v0, /device:TPU:8, one launch (start us, length us, event | category | flops | bytes accessed | tf_op | source)
XLA Modules:
  0.0 261.6 jit_solution(2452550016362452787)
XLA Ops:
  0.6 1.0 slice.424
  1.6 0.0 copy-start.2
  1.6 0.0 copy-start.1
  1.6 3.5 %collective-permute-start = (bf16[64,2048]{1,0:T(8,128)(2,1)S(1)}, bf16[64,2048]{1,0:T(8,128)(2,1)S(1)}, u32[]{:S(2)}, u32[]{:S(2)}) collective-permute-start(bf16[64,2048]{1,0:T(8,128)(2,1)S(1)} %slice.424), channel_id=1, source_target_pairs={{0,2},{2,4},{4,6},{6,8},{8,10},{10,12},{12,14},{14,16},{16,18},{18... | collective-permute-start | bytes 786440 | tf_op jit(solution)/shard_map/ppermute | solution.py:16
  5.2 6.2 %copy.67 = bf16[2,128,4096]{1,0,2:T(2,128)(2,1)} copy(bf16[2,128,4096]{2,1,0:T(8,128)(2,1)} %param.6) | data formatting | bytes 4194304 | tf_op args[1]
  11.3 0.0 copy-start
  11.3 3.9 %all-to-all-start = ((bf16[2,128,4096]{1,0,2:T(2,128)(2,1)}), bf16[2,128,4096]{1,0,2:T(2,128)(2,1)S(1)}, u32[]{:S(2)}, u32[]{:S(2)}) async-start(bf16[2,128,4096]{1,0,2:T(2,128)(2,1)} %copy.67), calls=%async_computation | async-start | bytes 4194304 | tf_op jit(solution)/shard_map/all_to_all | solution.py:113
  15.2 0.0 copy-done.2
  15.2 0.6 fusion.48
  18.4 0.0 copy-done.1
  18.4 0.1 copy.60
  18.5 0.2 negate_exponential_fusion
  18.8 0.1 copy.64
  18.9 0.0 all-to-all-done
  18.9 3.9 %copy.68 = bf16[2,128,2,2048]{3,1,2,0:T(8,128)(2,1)} copy(bf16[2,128,2,2048]{1,0,3,2:T(2,128)(2,1)S(1)} %bitcast.61) | data formatting | bytes 4194304 | tf_op jit(solution)/shard_map/all_to_all | solution.py:113
  22.8 0.0 collective-permute-done
  22.8 0.0 copy-done
  22.9 0.3 dynamic-slice_bitcast_fusion.1
  23.2 2.4 convolution_bitcast_fusion
  25.6 0.0 copy-start.3
  25.6 0.1 copy.69
  25.7 3.9 %all_to_all.64 = f32[2,256,128]{2,1,0:T(8,128)S(1)} all-to-all(f32[2,256,128]{2,1,0:T(8,128)S(1)} %broadcast_in_dim.76), channel_id=1, replica_groups=mesh['tm_0'=16,'tm_1'=4,'tm_2'=4,'state'=2] {'state'}, dimensions={0} | all-to-all | bytes 524288 | tf_op jit(solution)/shard_map/all_to_all | solution.py:21
  29.7 0.1 copy.89
  29.8 0.1 sqrt_multiply_fusion
  29.9 0.1 copy.91
  30.0 4.7 %multiply_reduce_fusion.1 = f32[128,128]{1,0:T(8,128)S(1)} fusion(f32[128,128]{1,0:T(8,128)S(1)} %copy.91, f32[128,128]{1,0:T(8,128)S(1)} %copy.64, pred[128,128]{1,0:T(8,128)(4,1)S(1)} %iota_compare_fusion), kind=kLoop, calls=%fused_computation.1 | loop fusion | flops 14663680 | bytes 212992
  34.7 0.1 copy.81
  34.8 0.7 broadcast_in_dim.77
  35.5 18.7 %all-to-all-start.2 = ((f32[64,1,256]{2,1,0:T(1,128)}), f32[64,1,256]{2,1,0:T(1,128)S(1)}, u32[]{:S(2)}, u32[]{:S(2)}) async-start(f32[64,1,256]{2,1,0:T(1,128)} %broadcast_in_dim.77), calls=%async_computation.2 | async-start | bytes 131072 | tf_op jit(solution)/shard_map/all_to_all | solution.py:21
  54.2 14.2 %all-to-all-done.2 = f32[64,1,256]{2,1,0:T(1,128)S(1)} async-done(((f32[64,1,256]{2,1,0:T(1,128)}), f32[64,1,256]{2,1,0:T(1,128)S(1)}, u32[]{:S(2)}, u32[]{:S(2)}) %all-to-all-start.2) | async-done | bytes 65568 | tf_op jit(solution)/shard_map/all_to_all | solution.py:21
  68.5 0.7 broadcast_in_dim.78
  69.2 4.0 %all-to-all-start.3 = ((f32[4,64,1,256]{3,1,2,0:T(8,128)}), f32[4,64,1,256]{3,1,2,0:T(8,128)S(1)}, u32[]{:S(2)}, u32[]{:S(2)}) async-start(f32[4,64,1,256]{3,1,2,0:T(8,128)} %broadcast_in_dim.78), calls=%async_computation.3 | async-start | bytes 524288 | tf_op jit(solution)/shard_map/all_to_all | solution.py:21
  73.2 0.0 copy-done.3
  73.2 6.7 %all-to-all-done.3 = f32[4,64,1,256]{3,1,2,0:T(8,128)S(1)} async-done(((f32[4,64,1,256]{3,1,2,0:T(8,128)}), f32[4,64,1,256]{3,1,2,0:T(8,128)S(1)}, u32[]{:S(2)}, u32[]{:S(2)}) %all-to-all-start.3) | async-done | bytes 262176 | tf_op jit(solution)/shard_map/all_to_all | solution.py:21
  79.9 0.2 copy.71
  80.1 0.1 reshape_reshape.9
  81.7 0.3 fusion.14
  81.9 0.1 copy.61
  82.0 0.1 copy.92
  82.2 4.7 %multiply_reduce_fusion = f32[128,128]{1,0:T(8,128)S(1)} fusion(f32[128,128]{1,0:T(8,128)S(1)} %copy.92, f32[128,128]{1,0:T(8,128)S(1)} %copy.61, pred[128,128]{1,0:T(8,128)(4,1)S(1)} %iota_compare_fusion.1), kind=kLoop, calls=%fused_computation | loop fusion | flops 14663680 | bytes 212992
  86.9 0.1 copy.86
  87.0 19.1 %all_to_all.65 = f32[64,1,256]{2,1,0:T(1,128)S(1)} all-to-all(f32[64,1,256]{2,1,0:T(1,128)S(1)} %broadcast_in_dim.80), channel_id=1, replica_groups=mesh['tm_0'=16,'tm_1'=4,'tm_2'=4,'state'=2] {'tm_0','tm_1'}, dimensions={0} | all-to-all | bytes 131072 | tf_op jit(solution)/shard_map/all_to_all | solution.py:21
  106.1 0.7 broadcast_in_dim.81
  106.8 3.4 %all-to-all-start.5 = ((f32[4,64,1,256]{3,1,2,0:T(8,128)}), f32[4,64,1,256]{3,1,2,0:T(8,128)S(1)}, u32[]{:S(2)}, u32[]{:S(2)}) async-start(f32[4,64,1,256]{3,1,2,0:T(8,128)} %broadcast_in_dim.81), calls=%async_computation.5 | async-start | bytes 524288 | tf_op jit(solution)/shard_map/all_to_all | solution.py:21
  110.3 6.6 %all-to-all-done.5 = f32[4,64,1,256]{3,1,2,0:T(8,128)S(1)} async-done(((f32[4,64,1,256]{3,1,2,0:T(8,128)}), f32[4,64,1,256]{3,1,2,0:T(8,128)S(1)}, u32[]{:S(2)}, u32[]{:S(2)}) %all-to-all-start.5) | async-done | bytes 262176 | tf_op jit(solution)/shard_map/all_to_all | solution.py:21
  116.9 0.2 copy.72
  117.1 0.1 reshape_reshape.10
  118.8 0.1 rev.2
  118.9 2.5 collective-permute-start.1
  121.4 5.1 %collective-permute-done.1 = f32[128,1]{0,1:T(1,128)S(1)} collective-permute-done((f32[128,1]{0,1:T(1,128)S(1)}, f32[128,1]{0,1:T(1,128)S(1)}, u32[]{:S(2)}, u32[]{:S(2)}) %collective-permute-start.1) | collective-permute-done | bytes 544 | tf_op jit(solution)/shard_map/ppermute | solution.py:16
  126.5 0.1 fusion.13
  126.5 0.1 copy.73
  126.7 3.8 %all_to_all.66 = bf16[2,128,128]{2,1,0:T(8,128)(2,1)S(1)} all-to-all(bf16[2,128,128]{2,1,0:T(8,128)(2,1)S(1)} %broadcast_in_dim.82), channel_id=1, replica_groups=mesh['tm_0'=16,'tm_1'=4,'tm_2'=4,'state'=2] {'state'}, dimensions={0} | all-to-all | bytes 131072 | tf_op jit(solution)/shard_map/all_to_all | solution.py:21
  130.4 0.4 fusion.5
  130.9 0.4 fusion.3
  131.3 2.4 pad_maximum_fusion
  133.8 5.4 %copy.74 = f32[2048,512]{1,0:T(8,128)} copy(f32[2048,512]{0,1:T(8,128)} %pad_maximum_fusion) | data formatting | bytes 8388608 | tf_op jit(solution)/shard_map/concatenate | solution.py:165
  139.2 2.8 %copy.75 = f32[4,64,8,512]{3,2,1,0:T(8,128)S(1)} copy(f32[4,64,8,512]{3,2,0,1:T(8,128)} %bitcast.60) | data formatting | bytes 8388608 | tf_op jit(solution)/shard_map/transpose | solution.py:55
  142.0 52.9 %all_to_all.67 = f32[4,64,8,512]{3,2,1,0:T(8,128)} all-to-all(f32[4,64,8,512]{3,2,1,0:T(8,128)S(1)} %copy.75), channel_id=1, replica_groups=mesh['tm_0'=16,'tm_1'=4,'tm_2'=4,'state'=2] {'tm_2'}, dimensions={0} | all-to-all | bytes 8388608 | tf_op jit(solution)/shard_map/all_to_all | solution.py:60
  194.9 3.8 %reduce_sum.28 = f32[64,8,512]{2,1,0:T(8,128)} reduce(f32[4,64,8,512]{3,2,1,0:T(8,128)} %all_to_all.67, f32[]{:T(128)} %constant.49.clone.1), dimensions={0}, to_apply=%region_1.2 | reduce | flops 786432 | bytes 5242884 | tf_op jit(solution)/shard_map/reduce_sum | solution.py:61
  198.7 7.5 %all-to-all-start.8 = ((f32[64,8,512]{2,1,0:T(8,128)}), f32[64,8,512]{2,1,0:T(8,128)S(1)}, u32[]{:S(2)}, u32[]{:S(2)}) async-start(f32[64,8,512]{2,1,0:T(8,128)} %reduce_sum.28), calls=%async_computation.8 | async-start | bytes 2097152 | tf_op jit(solution)/shard_map/all_to_all | solution.py:67
  206.2 0.7 copy.76
  206.9 54.0 %all-to-all-done.8 = f32[64,8,512]{2,1,0:T(8,128)S(1)} async-done(((f32[64,8,512]{2,1,0:T(8,128)}), f32[64,8,512]{2,1,0:T(8,128)S(1)}, u32[]{:S(2)}, u32[]{:S(2)}) %all-to-all-start.8) | async-done | bytes 1048608 | tf_op jit(solution)/shard_map/all_to_all | solution.py:67
  260.9 0.7 reduce_sum.29
  (211 shorter events, 2.5 us)
Async XLA Ops:
  1.6 13.6 %copy-start.2 = (s32[2]{0:T(128)S(1)}, s32[2]{0:T(128)}, u32[]{:S(2)}) copy-start(s32[2]{0:T(128)} %param.9) | copy-start | bytes 28
  1.6 16.8 %copy-start.1 = (f32[128,128]{1,0:T(8,128)S(1)}, f32[128,128]{1,0:T(8,128)}, u32[]{:S(2)}) copy-start(f32[128,128]{1,0:T(8,128)} %param.7) | copy-start | bytes 196612
  1.6 21.2 %collective-permute-start = (bf16[64,2048]{1,0:T(8,128)(2,1)S(1)}, bf16[64,2048]{1,0:T(8,128)(2,1)S(1)}, u32[]{:S(2)}, u32[]{:S(2)}) collective-permute-start(bf16[64,2048]{1,0:T(8,128)(2,1)S(1)} %slice.424), channel_id=1, source_target_pairs={{0,2},{2,4},{4,6},{6,8},{8,10},{10,12},{12,14},{14,16},{16,18},{18... | collective-permute-start | bytes 786440 | tf_op jit(solution)/shard_map/ppermute | solution.py:16
  11.3 11.5 %copy-start = (bf16[128,2048]{1,0:T(8,128)(2,1)S(1)}, bf16[128,2048]{1,0:T(8,128)(2,1)}, u32[]{:S(2)}) copy-start(bf16[128,2048]{1,0:T(8,128)(2,1)} %param.5) | copy-start | bytes 1572868
  11.3 7.6 %all-to-all-start = ((bf16[2,128,4096]{1,0,2:T(2,128)(2,1)}), bf16[2,128,4096]{1,0,2:T(2,128)(2,1)S(1)}, u32[]{:S(2)}, u32[]{:S(2)}) async-start(bf16[2,128,4096]{1,0,2:T(2,128)(2,1)} %copy.67), calls=%async_computation | async-start | bytes 4194304 | tf_op jit(solution)/shard_map/all_to_all | solution.py:113
  25.6 47.6 %copy-start.3 = (f32[128]{0:T(128)S(1)}, f32[128]{0:T(128)}, u32[]{:S(2)}) copy-start(f32[128]{0:T(128)} %param.8) | copy-start | bytes 1540
  35.5 33.0 %all-to-all-start.2 = ((f32[64,1,256]{2,1,0:T(1,128)}), f32[64,1,256]{2,1,0:T(1,128)S(1)}, u32[]{:S(2)}, u32[]{:S(2)}) async-start(f32[64,1,256]{2,1,0:T(1,128)} %broadcast_in_dim.77), calls=%async_computation.2 | async-start | bytes 131072 | tf_op jit(solution)/shard_map/all_to_all | solution.py:21
  69.2 10.7 %all-to-all-start.3 = ((f32[4,64,1,256]{3,1,2,0:T(8,128)}), f32[4,64,1,256]{3,1,2,0:T(8,128)S(1)}, u32[]{:S(2)}, u32[]{:S(2)}) async-start(f32[4,64,1,256]{3,1,2,0:T(8,128)} %broadcast_in_dim.78), calls=%async_computation.3 | async-start | bytes 524288 | tf_op jit(solution)/shard_map/all_to_all | solution.py:21
  106.8 10.1 %all-to-all-start.5 = ((f32[4,64,1,256]{3,1,2,0:T(8,128)}), f32[4,64,1,256]{3,1,2,0:T(8,128)S(1)}, u32[]{:S(2)}, u32[]{:S(2)}) async-start(f32[4,64,1,256]{3,1,2,0:T(8,128)} %broadcast_in_dim.81), calls=%async_computation.5 | async-start | bytes 524288 | tf_op jit(solution)/shard_map/all_to_all | solution.py:21
  118.9 7.5 %collective-permute-start.1 = (f32[128,1]{0,1:T(1,128)S(1)}, f32[128,1]{0,1:T(1,128)S(1)}, u32[]{:S(2)}, u32[]{:S(2)}) collective-permute-start(f32[128,1]{0,1:T(1,128)S(1)} %slice.587), channel_id=1, source_target_pairs={{0,2},{2,4},{4,6},{6,8},{8,10},{10,12},{12,14},{14,16},{16,18},{18... | collective-permute-start | bytes 1544 | tf_op jit(solution)/shard_map/ppermute | solution.py:16
  198.7 62.2 %all-to-all-start.8 = ((f32[64,8,512]{2,1,0:T(8,128)}), f32[64,8,512]{2,1,0:T(8,128)S(1)}, u32[]{:S(2)}, u32[]{:S(2)}) async-start(f32[64,8,512]{2,1,0:T(8,128)} %reduce_sum.28), calls=%async_computation.8 | async-start | bytes 2097152 | tf_op jit(solution)/shard_map/all_to_all | solution.py:67
where the time goes:
time: 263 us; the launch traced here: 262 us
  waiting for transfers between devices  86.6 us (33%)
  blocking collectives  79.7 us (30%)
  starting transfers between devices  43.5 us (17%)
  local copies, waits for them, and re-layouts  26.3 us (10%)
  other arithmetic  17.2 us (7%)
  between operations  4.56 us (2%)
  matrix products  3.8 us (1%)
    all_to_all x1, waiting for transfers between devices, sum_by_axis(): return jnp.sum(lax.all_to_all(own, far, 0, 0, tiled=True), axis=0)  54 us
    all_to_all x1, blocking collectives, summed_on_arrival(): blocks = lax.all_to_all(in_blocks(x, dim, peers), axis, 0, 0, tiled=True)  52.9 us
    all_to_all x3, waiting for transfers between devices, copy_for_each(): return lax.all_to_all(copies, axis, split_axis=0, concat_axis=0, tiled=True)  27.5 us
    all_to_all x3, blocking collectives, copy_for_each(): return lax.all_to_all(copies, axis, split_axis=0, concat_axis=0, tiled=True)  26.8 us
    all_to_all x3, starting transfers between devices, copy_for_each(): return lax.all_to_all(copies, axis, split_axis=0, concat_axis=0, tiled=True)  26.1 us
    unnamed x2, other arithmetic  9.43 us
    all_to_all x1, starting transfers between devices, sum_by_axis(): return jnp.sum(lax.all_to_all(own, far, 0, 0, tiled=True), axis=0)  7.47 us
    unnamed x17, local copies, waits for them, and re-layouts  7.29 us
  transfers between devices with their start and end apart: 7, of which 5 were waited for; matrix products, arithmetic and copies ran while one was open for 5% of the time, Pallas kernels for 0%

commit v1 on v0

--- a/solution.py
+++ b/solution.py
@@ -110,7 +110,10 @@
     local_taps = [
         lax.dynamic_slice_in_dim(local_rows, DMAX - dilation[k], frames, 0) for k in range(TAPS)
     ]
-    gain_cols = lax.all_to_all(gain, "state", split_axis=2, concat_axis=1, tiled=True)
+    y1 = lax.psum(1, axis_name="state")
+    g_now = jnp.stack(jnp.split(gain, y1, axis=2))
+    spare = lax.all_to_all(g_now, split_axis=0, axis_name="state", concat_axis=0)
+    gain_cols = jnp.concatenate(spare, axis=1)
     local_view = jnp.stack(local_taps, 1)
     partial_drive = jnp.einsum(
         "lky,khy->hl", local_view, gain_cols, preferred_element_type=jnp.float32

time: 263 us -> 257 us (0.977)
  local copies, waits for them, and re-layouts: 26.3 us -> 19.3 us
    unnamed x17 -> x16, local copies, waits for them, and re-layouts: 7.29 us -> 1.14 us
    all_to_all x1 -> x0, local copies, waits for them, and re-layouts: 3.88 us -> none  [per_device(): lax.all_to_all(gain, 'state', split_axis=2, concat_axis=1, tiled=True)]
  transfers between devices with their start and end apart: 7 -> 7, of which waited for: 5 -> 5; matrix products, arithmetic and copies ran while one was open for 5% -> 3% of each run, Pallas kernels for 0% -> 0%
where the time goes in v1:
time: 257 us; the launch traced here: 256 us
  waiting for transfers between devices  86.6 us (34%)
  blocking collectives  79.7 us (31%)
  starting transfers between devices  43.4 us (17%)
  local copies, waits for them, and re-layouts  19.3 us (8%)
  other arithmetic  18.7 us (7%)
  between operations  4.55 us (2%)
  matrix products  3.68 us (1%)
    all_to_all x1, waiting for transfers between devices, sum_by_axis(): return jnp.sum(lax.all_to_all(own, far, 0, 0, tiled=True), axis=0)  54 us
    all_to_all x1, blocking collectives, summed_on_arrival(): blocks = lax.all_to_all(in_blocks(x, dim, peers), axis, 0, 0, tiled=True)  52.9 us
    all_to_all x3, waiting for transfers between devices, copy_for_each(): return lax.all_to_all(copies, axis, split_axis=0, concat_axis=0, tiled=True)  27.5 us
    all_to_all x3, blocking collectives, copy_for_each(): return lax.all_to_all(copies, axis, split_axis=0, concat_axis=0, tiled=True)  26.8 us
    all_to_all x3, starting transfers between devices, copy_for_each(): return lax.all_to_all(copies, axis, split_axis=0, concat_axis=0, tiled=True)  26.1 us
    unnamed x2, other arithmetic  9.43 us
    all_to_all x1, starting transfers between devices, sum_by_axis(): return jnp.sum(lax.all_to_all(own, far, 0, 0, tiled=True), axis=0)  7.47 us
    ppermute x2, starting transfers between devices, from_behind(): return lax.ppermute(x, axis, pairs)  5.87 us
  transfers between devices with their start and end apart: 7, of which 5 were waited for; matrix products, arithmetic and copies ran while one was open for 3% of the time, Pallas kernels for 0%

profile of v1, /device:TPU:8, one launch (start us, length us, event | category | flops | bytes accessed | tf_op | source)
XLA Modules:
  0.0 255.9 jit_solution(9385085939151351410)
XLA Ops:
  0.6 1.0 slice.424
  1.6 3.4 %collective-permute-start = (bf16[64,2048]{1,0:T(8,128)(2,1)S(1)}, bf16[64,2048]{1,0:T(8,128)(2,1)S(1)}, u32[]{:S(2)}, u32[]{:S(2)}) collective-permute-start(bf16[64,2048]{1,0:T(8,128)(2,1)S(1)} %slice.424), channel_id=1, source_target_pairs={{0,2},{2,4},{4,6},{6,8},{8,10},{10,12},{12,14},{14,16},{16,18},{18... | collective-permute-start | bytes 786440 | tf_op jit(solution)/shard_map/ppermute | solution.py:16
  5.0 1.7 slice_bitcast_fusion.1
  6.7 0.0 copy-start.2
  6.7 0.0 copy-start.1
  6.7 1.5 pad_maximum_fusion.1
  8.2 0.0 copy-start
  8.2 3.9 %all-to-all-start = ((bf16[2,2,128,2048]{3,2,1,0:T(8,128)(2,1)}), bf16[2,2,128,2048]{3,2,1,0:T(8,128)(2,1)S(1)}, u32[]{:S(2)}, u32[]{:S(2)}) async-start(bf16[2,2,128,2048]{3,2,1,0:T(8,128)(2,1)} %pad_maximum_fusion.1), calls=%async_computation | async-start | bytes 4194304 | tf_op jit(solution)/shard_map/all_to_all | solution.py:115
  12.2 0.0 copy-done.2
  12.2 0.6 fusion.48
  15.3 0.0 copy-done.1
  15.4 0.1 copy.54
  15.5 0.2 negate_exponential_fusion
  15.7 0.1 copy.58
  15.8 0.0 all-to-all-done
  15.8 1.5 copy.61
  17.3 0.0 collective-permute-done
  17.4 0.0 copy-done
  17.4 0.3 dynamic-slice_bitcast_fusion.1
  17.7 2.3 convolution_bitcast_fusion
  20.0 0.0 copy-start.3
  20.0 3.9 %all_to_all.51 = f32[2,256,128]{2,1,0:T(8,128)S(1)} all-to-all(f32[2,256,128]{2,1,0:T(8,128)S(1)} %broadcast_in_dim.76), channel_id=1, replica_groups=mesh['tm_0'=16,'tm_1'=4,'tm_2'=4,'state'=2] {'state'}, dimensions={0} | all-to-all | bytes 524288 | tf_op jit(solution)/shard_map/all_to_all | solution.py:21
  24.0 0.1 copy.81
  24.1 0.1 sqrt_multiply_fusion
  24.2 0.1 copy.83
  24.3 4.7 %multiply_reduce_fusion.1 = f32[128,128]{1,0:T(8,128)S(1)} fusion(f32[128,128]{1,0:T(8,128)S(1)} %copy.83, f32[128,128]{1,0:T(8,128)S(1)} %copy.58, pred[128,128]{1,0:T(8,128)(4,1)S(1)} %iota_compare_fusion), kind=kLoop, calls=%fused_computation.1 | loop fusion | flops 14663680 | bytes 212992
  29.0 0.1 copy.73
  29.1 0.7 broadcast_in_dim.77
  29.8 18.7 %all-to-all-start.2 = ((f32[64,1,256]{2,1,0:T(1,128)}), f32[64,1,256]{2,1,0:T(1,128)S(1)}, u32[]{:S(2)}, u32[]{:S(2)}) async-start(f32[64,1,256]{2,1,0:T(1,128)} %broadcast_in_dim.77), calls=%async_computation.2 | async-start | bytes 131072 | tf_op jit(solution)/shard_map/all_to_all | solution.py:21
  48.5 14.2 %all-to-all-done.2 = f32[64,1,256]{2,1,0:T(1,128)S(1)} async-done(((f32[64,1,256]{2,1,0:T(1,128)}), f32[64,1,256]{2,1,0:T(1,128)S(1)}, u32[]{:S(2)}, u32[]{:S(2)}) %all-to-all-start.2) | async-done | bytes 65568 | tf_op jit(solution)/shard_map/all_to_all | solution.py:21
  62.8 0.7 broadcast_in_dim.78
  63.5 4.0 %all-to-all-start.3 = ((f32[4,64,1,256]{3,1,2,0:T(8,128)}), f32[4,64,1,256]{3,1,2,0:T(8,128)S(1)}, u32[]{:S(2)}, u32[]{:S(2)}) async-start(f32[4,64,1,256]{3,1,2,0:T(8,128)} %broadcast_in_dim.78), calls=%async_computation.3 | async-start | bytes 524288 | tf_op jit(solution)/shard_map/all_to_all | solution.py:21
  67.5 0.0 copy-done.3
  67.5 6.7 %all-to-all-done.3 = f32[4,64,1,256]{3,1,2,0:T(8,128)S(1)} async-done(((f32[4,64,1,256]{3,1,2,0:T(8,128)}), f32[4,64,1,256]{3,1,2,0:T(8,128)S(1)}, u32[]{:S(2)}, u32[]{:S(2)}) %all-to-all-start.3) | async-done | bytes 262176 | tf_op jit(solution)/shard_map/all_to_all | solution.py:21
  74.2 0.2 copy.63
  74.4 0.1 reshape_reshape.9
  76.0 0.3 fusion.14
  76.3 0.1 copy.55
  76.3 0.1 copy.84
  76.5 4.7 %multiply_reduce_fusion = f32[128,128]{1,0:T(8,128)S(1)} fusion(f32[128,128]{1,0:T(8,128)S(1)} %copy.84, f32[128,128]{1,0:T(8,128)S(1)} %copy.55, pred[128,128]{1,0:T(8,128)(4,1)S(1)} %iota_compare_fusion.1), kind=kLoop, calls=%fused_computation | loop fusion | flops 14663680 | bytes 212992
  81.2 0.1 copy.78
  81.4 19.1 %all_to_all.52 = f32[64,1,256]{2,1,0:T(1,128)S(1)} all-to-all(f32[64,1,256]{2,1,0:T(1,128)S(1)} %broadcast_in_dim.80), channel_id=1, replica_groups=mesh['tm_0'=16,'tm_1'=4,'tm_2'=4,'state'=2] {'tm_0','tm_1'}, dimensions={0} | all-to-all | bytes 131072 | tf_op jit(solution)/shard_map/all_to_all | solution.py:21
  100.4 0.7 broadcast_in_dim.81
  101.2 3.4 %all-to-all-start.5 = ((f32[4,64,1,256]{3,1,2,0:T(8,128)}), f32[4,64,1,256]{3,1,2,0:T(8,128)S(1)}, u32[]{:S(2)}, u32[]{:S(2)}) async-start(f32[4,64,1,256]{3,1,2,0:T(8,128)} %broadcast_in_dim.81), calls=%async_computation.5 | async-start | bytes 524288 | tf_op jit(solution)/shard_map/all_to_all | solution.py:21
  104.6 6.6 %all-to-all-done.5 = f32[4,64,1,256]{3,1,2,0:T(8,128)S(1)} async-done(((f32[4,64,1,256]{3,1,2,0:T(8,128)}), f32[4,64,1,256]{3,1,2,0:T(8,128)S(1)}, u32[]{:S(2)}, u32[]{:S(2)}) %all-to-all-start.5) | async-done | bytes 262176 | tf_op jit(solution)/shard_map/all_to_all | solution.py:21
  111.2 0.2 copy.64
  111.4 0.1 reshape_reshape.10
  113.1 0.1 rev.2
  113.3 2.5 collective-permute-start.1
  115.7 5.1 %collective-permute-done.1 = f32[128,1]{0,1:T(1,128)S(1)} collective-permute-done((f32[128,1]{0,1:T(1,128)S(1)}, f32[128,1]{0,1:T(1,128)S(1)}, u32[]{:S(2)}, u32[]{:S(2)}) %collective-permute-start.1) | collective-permute-done | bytes 544 | tf_op jit(solution)/shard_map/ppermute | solution.py:16
  120.8 0.1 fusion.13
  120.9 0.1 copy.65
  121.0 3.8 %all_to_all.53 = bf16[2,128,128]{2,1,0:T(8,128)(2,1)S(1)} all-to-all(bf16[2,128,128]{2,1,0:T(8,128)(2,1)S(1)} %broadcast_in_dim.82), channel_id=1, replica_groups=mesh['tm_0'=16,'tm_1'=4,'tm_2'=4,'state'=2] {'state'}, dimensions={0} | all-to-all | bytes 131072 | tf_op jit(solution)/shard_map/all_to_all | solution.py:21
  124.8 0.4 fusion.5
  125.2 0.4 fusion.3
  125.7 2.4 pad_maximum_fusion
  128.1 5.5 %copy.66 = f32[2048,512]{1,0:T(8,128)} copy(f32[2048,512]{0,1:T(8,128)} %pad_maximum_fusion) | data formatting | bytes 8388608 | tf_op jit(solution)/shard_map/concatenate | solution.py:168
  133.6 2.8 %copy.67 = f32[4,64,8,512]{3,2,1,0:T(8,128)S(1)} copy(f32[4,64,8,512]{3,2,0,1:T(8,128)} %bitcast.60) | data formatting | bytes 8388608 | tf_op jit(solution)/shard_map/transpose | solution.py:55
  136.4 52.9 %all_to_all.54 = f32[4,64,8,512]{3,2,1,0:T(8,128)} all-to-all(f32[4,64,8,512]{3,2,1,0:T(8,128)S(1)} %copy.67), channel_id=1, replica_groups=mesh['tm_0'=16,'tm_1'=4,'tm_2'=4,'state'=2] {'tm_2'}, dimensions={0} | all-to-all | bytes 8388608 | tf_op jit(solution)/shard_map/all_to_all | solution.py:60
  189.3 3.8 %reduce_sum.28 = f32[64,8,512]{2,1,0:T(8,128)} reduce(f32[4,64,8,512]{3,2,1,0:T(8,128)} %all_to_all.54, f32[]{:T(128)} %constant.49.clone.1), dimensions={0}, to_apply=%region_1.2 | reduce | flops 786432 | bytes 5242884 | tf_op jit(solution)/shard_map/reduce_sum | solution.py:61
  193.0 7.5 %all-to-all-start.8 = ((f32[64,8,512]{2,1,0:T(8,128)}), f32[64,8,512]{2,1,0:T(8,128)S(1)}, u32[]{:S(2)}, u32[]{:S(2)}) async-start(f32[64,8,512]{2,1,0:T(8,128)} %reduce_sum.28), calls=%async_computation.8 | async-start | bytes 2097152 | tf_op jit(solution)/shard_map/all_to_all | solution.py:67
  200.5 0.7 copy.68
  201.3 54.0 %all-to-all-done.8 = f32[64,8,512]{2,1,0:T(8,128)S(1)} async-done(((f32[64,8,512]{2,1,0:T(8,128)}), f32[64,8,512]{2,1,0:T(8,128)S(1)}, u32[]{:S(2)}, u32[]{:S(2)}) %all-to-all-start.8) | async-done | bytes 1048608 | tf_op jit(solution)/shard_map/all_to_all | solution.py:67
  255.2 0.7 reduce_sum.29
  (211 shorter events, 2.5 us)
Async XLA Ops:
  1.6 15.7 %collective-permute-start = (bf16[64,2048]{1,0:T(8,128)(2,1)S(1)}, bf16[64,2048]{1,0:T(8,128)(2,1)S(1)}, u32[]{:S(2)}, u32[]{:S(2)}) collective-permute-start(bf16[64,2048]{1,0:T(8,128)(2,1)S(1)} %slice.424), channel_id=1, source_target_pairs={{0,2},{2,4},{4,6},{6,8},{8,10},{10,12},{12,14},{14,16},{16,18},{18... | collective-permute-start | bytes 786440 | tf_op jit(solution)/shard_map/ppermute | solution.py:16
  6.7 5.5 %copy-start.2 = (s32[2]{0:T(128)S(1)}, s32[2]{0:T(128)}, u32[]{:S(2)}) copy-start(s32[2]{0:T(128)} %param.9) | copy-start | bytes 28
  6.7 8.6 %copy-start.1 = (f32[128,128]{1,0:T(8,128)S(1)}, f32[128,128]{1,0:T(8,128)}, u32[]{:S(2)}) copy-start(f32[128,128]{1,0:T(8,128)} %param.7) | copy-start | bytes 196612
  8.2 9.1 %copy-start = (bf16[128,2048]{1,0:T(8,128)(2,1)S(1)}, bf16[128,2048]{1,0:T(8,128)(2,1)}, u32[]{:S(2)}) copy-start(bf16[128,2048]{1,0:T(8,128)(2,1)} %param.5) | copy-start | bytes 1572868
  8.2 7.6 %all-to-all-start = ((bf16[2,2,128,2048]{3,2,1,0:T(8,128)(2,1)}), bf16[2,2,128,2048]{3,2,1,0:T(8,128)(2,1)S(1)}, u32[]{:S(2)}, u32[]{:S(2)}) async-start(bf16[2,2,128,2048]{3,2,1,0:T(8,128)(2,1)} %pad_maximum_fusion.1), calls=%async_computation | async-start | bytes 4194304 | tf_op jit(solution)/shard_map/all_to_all | solution.py:115
  20.0 47.5 %copy-start.3 = (f32[128]{0:T(128)S(1)}, f32[128]{0:T(128)}, u32[]{:S(2)}) copy-start(f32[128]{0:T(128)} %param.8) | copy-start | bytes 1540
  29.8 33.0 %all-to-all-start.2 = ((f32[64,1,256]{2,1,0:T(1,128)}), f32[64,1,256]{2,1,0:T(1,128)S(1)}, u32[]{:S(2)}, u32[]{:S(2)}) async-start(f32[64,1,256]{2,1,0:T(1,128)} %broadcast_in_dim.77), calls=%async_computation.2 | async-start | bytes 131072 | tf_op jit(solution)/shard_map/all_to_all | solution.py:21
  63.5 10.7 %all-to-all-start.3 = ((f32[4,64,1,256]{3,1,2,0:T(8,128)}), f32[4,64,1,256]{3,1,2,0:T(8,128)S(1)}, u32[]{:S(2)}, u32[]{:S(2)}) async-start(f32[4,64,1,256]{3,1,2,0:T(8,128)} %broadcast_in_dim.78), calls=%async_computation.3 | async-start | bytes 524288 | tf_op jit(solution)/shard_map/all_to_all | solution.py:21
  101.2 10.1 %all-to-all-start.5 = ((f32[4,64,1,256]{3,1,2,0:T(8,128)}), f32[4,64,1,256]{3,1,2,0:T(8,128)S(1)}, u32[]{:S(2)}, u32[]{:S(2)}) async-start(f32[4,64,1,256]{3,1,2,0:T(8,128)} %broadcast_in_dim.81), calls=%async_computation.5 | async-start | bytes 524288 | tf_op jit(solution)/shard_map/all_to_all | solution.py:21
  113.3 7.5 %collective-permute-start.1 = (f32[128,1]{0,1:T(1,128)S(1)}, f32[128,1]{0,1:T(1,128)S(1)}, u32[]{:S(2)}, u32[]{:S(2)}) collective-permute-start(f32[128,1]{0,1:T(1,128)S(1)} %slice.587), channel_id=1, source_target_pairs={{0,2},{2,4},{4,6},{6,8},{8,10},{10,12},{12,14},{14,16},{16,18},{18... | collective-permute-start | bytes 1544 | tf_op jit(solution)/shard_map/ppermute | solution.py:16
  193.0 62.2 %all-to-all-start.8 = ((f32[64,8,512]{2,1,0:T(8,128)}), f32[64,8,512]{2,1,0:T(8,128)S(1)}, u32[]{:S(2)}, u32[]{:S(2)}) async-start(f32[64,8,512]{2,1,0:T(8,128)} %reduce_sum.28), calls=%async_computation.8 | async-start | bytes 2097152 | tf_op jit(solution)/shard_map/all_to_all | solution.py:67
